TPU v7x, 32 devices: a whole 2x2x4 slice. The times are simulated.
32 devices in a mesh: groups: 2 (over y), frame: 4 (over z), quarter: 2 (over x), sub: 2 (over core).
Axes of the slice: x: 2, y: 2, z: 4, core: 2. Of those that a mesh axis runs over, the one named last changes fastest.
Arguments:
- queries: bfloat16 [16, 1024, 256], P(('groups', 'frame'), ('quarter', 'sub')), parts along dimension 0, may hold values from -36 to 36
- keys: bfloat16 [16, 1024, 256], P(('groups', 'frame'), ('quarter', 'sub')), parts along dimension 0, may hold values from -6 to 6
- values: bfloat16 [16, 1024, 256], P(('groups', 'frame'), ('quarter', 'sub')), parts along dimension 0, may hold values from -6 to 6
Outputs:
- attended: bfloat16 [16, 1024, 256], P(('groups', 'frame'), ('quarter', 'sub')), parts along dimension 0
There are 2 independent parts, one for each index of `groups`. A program takes and returns all parts, laid end to end along the dimension named above; each array names one. Nothing has to cross between parts.
All inputs are finite; a program needn't handle non-finite values.
Results may differ from a plain program's by a relative error of at most 0.0028.
Values may be sent and summed in bfloat16 or wider, within the bound.
A program may use at most 64 MiB of HBM per device.

v0:
```python
import math
import jax
import jax.numpy as jnp
from jax import lax
from jax.sharding import PartitionSpec as P

STRIP = 16


def partial_attend(query_rows, key_rows, value_rows, running, score_scale):
    top_run, sum_run, acc_run = running
    scores = (
        jnp.einsum("frd,fnd->frn", query_rows, key_rows, preferred_element_type=jnp.float32)
        * score_scale
    )
    highest = jnp.maximum(top_run, jnp.max(scores, axis=-1, keepdims=True))
    expo = jnp.exp(scores - highest)
    factor = jnp.exp(top_run - highest)
    sum_next = sum_run * factor + jnp.sum(expo, axis=-1, keepdims=True)
    acc_next = acc_run * factor + jnp.einsum(
        "frn,fnd->frd", expo.astype(jnp.bfloat16), value_rows, preferred_element_type=jnp.float32
    )
    return (highest, sum_next, acc_next)


def fold_keys(query_rows, score_scale, running, pieces):
    key_piece, value_piece = pieces
    length = key_piece.shape[1]
    block_keys = math.gcd(length, 2048)
    for block_index in range(length // block_keys):
        lower = block_index * block_keys
        running = partial_attend(
            query_rows,
            key_piece[:, lower : lower + block_keys],
            value_piece[:, lower : lower + block_keys],
            running,
            score_scale,
        )
    return running


def empty_state(query_rows):
    frames_here, rows_here, width = query_rows.shape
    return (
        jnp.full((frames_here, rows_here, 1), -jnp.inf, jnp.float32),
        jnp.zeros((frames_here, rows_here, 1), jnp.float32),
        jnp.zeros((frames_here, rows_here, width), jnp.float32),
    )


def body(queries, keys, values):
    head_width = queries.shape[2] // 2
    frames_dev = queries.shape[0]
    tokens_dev = queries.shape[1]
    score_scale = 1.0 / math.sqrt(head_width)
    query_spatial = queries[:, :, :head_width]
    key_spatial = keys[:, :, :head_width]
    value_spatial = values[:, :, :head_width]
    frame_count = lax.axis_size("frame")
    local_strips = tokens_dev // (STRIP * frame_count)

    def to_strips(array):
        part_two = array[:, :, head_width:].reshape(
            frames_dev, frame_count, local_strips, STRIP, head_width
        )
        return part_two.transpose(1, 2, 0, 3, 4)

    query_strip = lax.all_to_all(
        to_strips(queries), "frame", split_axis=0, concat_axis=2, tiled=True
    )
    key_strip = lax.all_to_all(to_strips(keys), "frame", split_axis=0, concat_axis=2, tiled=True)
    value_strip = lax.all_to_all(
        to_strips(values), "frame", split_axis=0, concat_axis=2, tiled=True
    )
    item_count = query_strip.shape[1]
    frames_all = query_strip.shape[2]
    rows_strip = frames_all * STRIP
    query_flat = query_strip.reshape(item_count, rows_strip, head_width)
    key_flat = key_strip.reshape(item_count, rows_strip, head_width)
    value_flat = value_strip.reshape(item_count, rows_strip, head_width)
    scores = (
        jnp.einsum("nqd,nkd->nqk", query_flat, key_flat, preferred_element_type=jnp.float32)
        * score_scale
    )
    highest = jnp.max(scores, axis=-1, keepdims=True)
    expo = jnp.exp(scores - highest)
    totals = jnp.sum(expo, axis=-1, keepdims=True)
    mixed = jnp.einsum(
        "nqk,nkd->nqd", expo.astype(jnp.bfloat16), value_flat, preferred_element_type=jnp.float32
    )
    strip_out = (
        (mixed / totals).astype(jnp.bfloat16).reshape(1, item_count, frames_all, STRIP, head_width)
    )
    returned = lax.all_to_all(strip_out, "frame", split_axis=2, concat_axis=0, tiled=True)
    temporal = returned.transpose(2, 0, 1, 3, 4).reshape(frames_dev, tokens_dev, head_width)
    top_all, total_spatial, acc_spatial = fold_keys(
        query_spatial,
        score_scale,
        empty_state(query_spatial),
        (
            lax.all_gather(key_spatial, ("quarter", "sub"), axis=1, tiled=True),
            lax.all_gather(value_spatial, ("quarter", "sub"), axis=1, tiled=True),
        ),
    )
    spatial = (acc_spatial / total_spatial).astype(jnp.bfloat16)
    return jnp.concatenate([spatial, temporal], axis=-1)


def solution(mesh):
    in_specs = (
        P(("groups", "frame"), ("quarter", "sub"), None),
        P(("groups", "frame"), ("quarter", "sub"), None),
        P(("groups", "frame"), ("quarter", "sub"), None),
    )
    out_specs = P(("groups", "frame"), ("quarter", "sub"), None)
    return jax.shard_map(body, mesh=mesh, in_specs=in_specs, out_specs=out_specs, check_vma=False)
```

profile of v0, /device:TPU:0, one launch (start us, length us, event | category | flops | bytes accessed | tf_op | source)
XLA Modules:
  0.0 53.8 jit_solution(1499810248122373728)
XLA Ops:
  0.0 1.0 %fusion.16 = (bf16[2,256,128]{2,1,0:T(8,128)(2,1)S(1)}, bf16[2,256,128]{2,1,0:T(8,128)(2,1)S(1)}) fusion(bf16[2,256,256]{2,1,0:T(8,128)(2,1)} %param.4), kind=kLoop, calls=%fused_computation.22 | loop fusion | bytes 524288 | tf_op jit(solution)/shard_map/slice | solution.py:57
  1.0 0.0 copy-start
  1.0 0.7 %copy.31 = bf16[4,4,2,16,128]{4,3,2,1,0:T(8,128)(2,1)} copy(bf16[4,4,2,16,128]{4,3,1,0,2:T(8,128)(2,1)S(1)} %bitcast.42) | data formatting | bytes 262144 | tf_op jit(solution)/shard_map/transpose | solution.py:66
  1.7 6.3 %all-to-all-start.1 = ((bf16[4,4,2,16,128]{4,3,2,1,0:T(8,128)(2,1)}), bf16[4,4,2,16,128]{4,3,2,1,0:T(8,128)(2,1)S(1)}, u32[]{:S(2)}, u32[]{:S(2)}) async-start(bf16[4,4,2,16,128]{4,3,2,1,0:T(8,128)(2,1)} %copy.31), calls=%async_computation.1 | async-start | bytes 262144 | tf_op jit(solution)/shard_map/all_to_all | solution.py:71
  8.0 7.3 %all_gather.6 = bf16[2,1024,128]{2,1,0:T(8,128)(2,1)S(1)} all-gather(bf16[2,256,128]{2,1,0:T(8,128)(2,1)S(1)} %get-tuple-element.5), channel_id=1, replica_groups=mesh['groups'=2,'frame'=4,'quarter'=2,'sub'=2] {'quarter','sub'}, dimensions={1}, use_global_device_ids=true | all-gather | bytes 655360 | tf_op jit(solution)/shard_map/all_gather | solution.py:101
  15.3 1.4 %multiply_reduce_fusion = (f32[2,256]{1,0:T(2,128)S(1)}, f32[2,256,1024]{2,1,0:T(8,128)S(1)}) fusion(bf16[2,1024,128]{2,1,0:T(8,128)(2,1)S(1)} %all_gather.6, bf16[2,256,256]{2,1,0:T(8,128)(2,1)} %param.3), kind=kOutput, calls=%fused_computation.1 | convolution fusion | flops 135265792 | bytes 2754560 | tf_op jit(solution)/shard_map/frd,fnd->frn/dot_general | solution.py:13
  16.8 0.1 copy.43
  16.9 0.7 %copy.29 = bf16[4,4,2,16,128]{4,3,2,1,0:T(8,128)(2,1)} copy(bf16[4,4,2,16,128]{4,3,1,0,2:T(8,128)(2,1)S(1)} %bitcast.37) | data formatting | bytes 262144 | tf_op jit(solution)/shard_map/transpose | solution.py:66
  17.6 0.7 %copy.33 = bf16[4,4,2,16,128]{4,3,2,1,0:T(8,128)(2,1)} copy(bf16[4,4,2,16,128]{4,3,1,0,2:T(8,128)(2,1)S(1)} %bitcast.41) | data formatting | bytes 262144 | tf_op jit(solution)/shard_map/transpose | solution.py:66
  18.2 0.5 fusion
  18.7 0.0 all-to-all-done.1
  18.7 5.1 %all-to-all-start = ((bf16[4,4,2,16,128]{4,3,2,1,0:T(8,128)(2,1)}), bf16[4,4,2,16,128]{4,3,2,1,0:T(8,128)(2,1)S(1)}, u32[]{:S(2)}, u32[]{:S(2)}) async-start(bf16[4,4,2,16,128]{4,3,2,1,0:T(8,128)(2,1)} %copy.29), calls=%async_computation | async-start | bytes 262144 | tf_op jit(solution)/shard_map/all_to_all | solution.py:68
  23.9 6.4 %all-to-all-done = bf16[4,4,2,16,128]{4,3,2,1,0:T(8,128)(2,1)S(1)} async-done(((bf16[4,4,2,16,128]{4,3,2,1,0:T(8,128)(2,1)}), bf16[4,4,2,16,128]{4,3,2,1,0:T(8,128)(2,1)S(1)}, u32[]{:S(2)}, u32[]{:S(2)}) %all-to-all-start) | async-done | bytes 131104 | tf_op jit(solution)/shard_map/all_to_all | solution.py:68
  30.3 3.3 %all-to-all-start.2 = ((bf16[4,4,2,16,128]{4,3,2,1,0:T(8,128)(2,1)}), bf16[4,4,2,16,128]{4,3,2,1,0:T(8,128)(2,1)S(1)}, u32[]{:S(2)}, u32[]{:S(2)}) async-start(bf16[4,4,2,16,128]{4,3,2,1,0:T(8,128)(2,1)} %copy.33), calls=%async_computation.2 | async-start | bytes 262144 | tf_op jit(solution)/shard_map/all_to_all | solution.py:72
  33.6 6.5 %all_gather.7 = bf16[2,1024,128]{1,2,0:T(8,128)(2,1)S(1)} all-gather(bf16[2,256,128]{1,2,0:T(8,128)(2,1)S(1)} %copy.43), channel_id=1, replica_groups=mesh['groups'=2,'frame'=4,'quarter'=2,'sub'=2] {'quarter','sub'}, dimensions={1}, use_global_device_ids=true | all-gather | bytes 655360 | tf_op jit(solution)/shard_map/all_gather | solution.py:102
  40.2 0.2 fusion.18
  40.4 0.1 fusion.8
  40.5 0.3 fusion.3
  40.7 0.7 %copy.36 = bf16[1,4,8,16,128]{4,3,1,0,2:T(8,128)(2,1)} copy(bf16[1,4,8,16,128]{4,3,2,1,0:T(8,128)(2,1)S(1)} %bitcast.44) | data formatting | bytes 262144 | tf_op jit(solution)/shard_map/reshape | solution.py:92
  41.4 5.0 %all-to-all-start.3 = ((bf16[1,4,8,16,128]{4,3,1,0,2:T(8,128)(2,1)}), bf16[1,4,8,16,128]{4,3,1,0,2:T(8,128)(2,1)S(1)}, u32[]{:S(2)}, u32[]{:S(2)}) async-start(bf16[1,4,8,16,128]{4,3,1,0,2:T(8,128)(2,1)} %copy.36), calls=%async_computation.3 | async-start | bytes 262144 | tf_op jit(solution)/shard_map/all_to_all | solution.py:94
  46.4 0.6 %fusion.4 = bf16[2,256,128]{1,2,0:T(8,128)(2,1)S(1)} fusion(bf16[2,1024,128]{1,2,0:T(8,128)(2,1)S(1)} %all_gather.7, f32[2,256,1024]{2,1,0:T(8,128)S(1)} %get-tuple-element.14, f32[2,256]{1,0:T(2,128)S(1)} %get-tuple-element.13, f32[2,256]{1,0:T(2,128)S(1)} %get-tuple-element.10, f32[2,256]{1,0:T(2,128)S(1)} %get-tuple-element.9), kind=kOutput, calls=%fused_computation.9 | convolution fusion | flops 135987200 | bytes 2758656 | tf_op jit(solution)/shard_map/frn,fnd->frd/dot_general | solution.py:20
  47.0 5.8 %all-to-all-done.3 = bf16[1,4,8,16,128]{4,3,1,0,2:T(8,128)(2,1)S(1)} async-done(((bf16[1,4,8,16,128]{4,3,1,0,2:T(8,128)(2,1)}), bf16[1,4,8,16,128]{4,3,1,0,2:T(8,128)(2,1)S(1)}, u32[]{:S(2)}, u32[]{:S(2)}) %all-to-all-start.3) | async-done | bytes 131104 | tf_op jit(solution)/shard_map/all_to_all | solution.py:94
  52.9 0.1 copy.39
  53.0 0.8 %copy.40 = bf16[2,256,256]{2,1,0:T(8,128)(2,1)} copy(bf16[2,256,256]{1,2,0:T(8,128)(2,1)S(1)} %pad_maximum_fusion) | data formatting | bytes 524288 | tf_op jit(solution)/shard_map/concatenate | solution.py:106
  (11 shorter events, 0.1 us)
Async XLA Ops:
  1.0 15.7 %copy-start = (bf16[2,256,256]{2,1,0:T(8,128)(2,1)S(1)}, bf16[2,256,256]{2,1,0:T(8,128)(2,1)}, u32[]{:S(2)}) copy-start(bf16[2,256,256]{2,1,0:T(8,128)(2,1)} %param.5) | copy-start | bytes 786436
  1.7 17.1 %all-to-all-start.1 = ((bf16[4,4,2,16,128]{4,3,2,1,0:T(8,128)(2,1)}), bf16[4,4,2,16,128]{4,3,2,1,0:T(8,128)(2,1)S(1)}, u32[]{:S(2)}, u32[]{:S(2)}) async-start(bf16[4,4,2,16,128]{4,3,2,1,0:T(8,128)(2,1)} %copy.31), calls=%async_computation.1 | async-start | bytes 262144 | tf_op jit(solution)/shard_map/all_to_all | solution.py:71
  8.0 8.9 %slice-start = ((bf16[2,256,256]{2,1,0:T(8,128)(2,1)}), bf16[2,256,128]{2,1,0:T(8,128)(2,1)S(1)}, s32[]{:S(2)}) async-start(bf16[2,256,256]{2,1,0:T(8,128)(2,1)} %param.3), calls=%async_computation.4 | async-start | bytes 262144 | tf_op jit(solution)/shard_map/slice | solution.py:63
  18.7 11.5 %all-to-all-start = ((bf16[4,4,2,16,128]{4,3,2,1,0:T(8,128)(2,1)}), bf16[4,4,2,16,128]{4,3,2,1,0:T(8,128)(2,1)S(1)}, u32[]{:S(2)}, u32[]{:S(2)}) async-start(bf16[4,4,2,16,128]{4,3,2,1,0:T(8,128)(2,1)} %copy.29), calls=%async_computation | async-start | bytes 262144 | tf_op jit(solution)/shard_map/all_to_all | solution.py:68
  30.3 9.9 %all-to-all-start.2 = ((bf16[4,4,2,16,128]{4,3,2,1,0:T(8,128)(2,1)}), bf16[4,4,2,16,128]{4,3,2,1,0:T(8,128)(2,1)S(1)}, u32[]{:S(2)}, u32[]{:S(2)}) async-start(bf16[4,4,2,16,128]{4,3,2,1,0:T(8,128)(2,1)} %copy.33), calls=%async_computation.2 | async-start | bytes 262144 | tf_op jit(solution)/shard_map/all_to_all | solution.py:72
  41.4 11.5 %all-to-all-start.3 = ((bf16[1,4,8,16,128]{4,3,1,0,2:T(8,128)(2,1)}), bf16[1,4,8,16,128]{4,3,1,0,2:T(8,128)(2,1)S(1)}, u32[]{:S(2)}, u32[]{:S(2)}) async-start(bf16[1,4,8,16,128]{4,3,1,0,2:T(8,128)(2,1)} %copy.36), calls=%async_computation.3 | async-start | bytes 262144 | tf_op jit(solution)/shard_map/all_to_all | solution.py:94
where the time goes:
time: 54.4 us; the launch traced here: 53.8 us
  starting transfers between devices  19.8 us (36%)
  blocking collectives  13.8 us (25%)
  waiting for transfers between devices  12.2 us (22%)
  local copies, waits for them, and re-layouts  4.8 us (9%)
  matrix products  2.5 us (5%)
  other arithmetic  0.58 us (1%)
    all_gather x1, blocking collectives, body(): lax.all_gather(key_spatial, ('quarter', 'sub'), axis=1, tiled=True)  7.29 us
    all_gather x1, blocking collectives, body(): lax.all_gather(value_spatial, ('quarter', 'sub'), axis=1, tiled=True)  6.5 us
    all_to_all x1, waiting for transfers between devices, body(): lax.all_to_all(to_strips(queries), 'frame', split_axis=0, concat_axis=2,...  6.41 us
    all_to_all x1, starting transfers between devices, body(): lax.all_to_all(to_strips(keys), 'frame', split_axis=0, concat_axis=2, til...  6.35 us
    all_to_all x1, waiting for transfers between devices, body(): lax.all_to_all(strip_out, 'frame', split_axis=2, concat_axis=0, tiled=True)  5.8 us
    all_to_all x1, starting transfers between devices, body(): lax.all_to_all(to_strips(queries), 'frame', split_axis=0, concat_axis=2,...  5.1 us
    all_to_all x1, starting transfers between devices, body(): lax.all_to_all(strip_out, 'frame', split_axis=2, concat_axis=0, tiled=True)  5.04 us
    all_to_all x1, starting transfers between devices, body(): lax.all_to_all(to_strips(values), 'frame', split_axis=0, concat_axis=2, t...  3.33 us
  transfers between devices with their start and end apart: 4, of which 2 were waited for; matrix products, arithmetic and copies ran while one was open for 7% of the time, Pallas kernels for 0%

commit v1 on v0

--- a/solution.py
+++ b/solution.py
@@ -5,6 +5,18 @@
 from jax.sharding import PartitionSpec as P
 
 STRIP = 16
+
+
+def gather_around(value, axis, dim):
+    ways, here, step = (lax.axis_size(axis), lax.axis_index(axis), value.shape[dim])
+    shape = [n * ways if d == dim else n for d, n in enumerate(value.shape)]
+    full = lax.dynamic_update_slice_in_dim(
+        jnp.zeros(shape, value.dtype), value, here * step, axis=dim
+    )
+    for far in range(1, ways):
+        value = lax.ppermute(value, axis, [(d, (d + 1) % ways) for d in range(ways)])
+        full = lax.dynamic_update_slice_in_dim(full, value, (here - far) % ways * step, axis=dim)
+    return full
 
 
 def partial_attend(query_rows, key_rows, value_rows, running, score_scale):
@@ -98,7 +110,7 @@
         score_scale,
         empty_state(query_spatial),
         (
-            lax.all_gather(key_spatial, ("quarter", "sub"), axis=1, tiled=True),
+            gather_around(key_spatial, ("quarter", "sub"), 1),
             lax.all_gather(value_spatial, ("quarter", "sub"), axis=1, tiled=True),
         ),
     )

time: 54.4 us -> 49.9 us (0.917)
  blocking collectives: 13.8 us -> 7.17 us
  waiting for transfers between devices: 12.2 us -> 15.6 us
  starting transfers between devices: 19.8 us -> 18.6 us
  local copies, waits for them, and re-layouts: 4.8 us -> 5.93 us
  matrix products: 2.5 us -> 1.43 us
    all_gather x1 -> x0, blocking collectives: 7.29 us -> none  [body(): lax.all_gather(key_spatial, ('quarter', 'sub'), axis=1, tiled=True)]
    all_to_all x1, waiting for transfers between devices: 0.01 us -> 6.22 us  [body(): lax.all_to_all(to_strips(values), 'frame', split_axis=0, concat_axis=2, t...]
    all_to_all x1, starting transfers between devices: 6.35 us -> 3.32 us  [body(): lax.all_to_all(to_strips(keys), 'frame', split_axis=0, concat_axis=2, til...]
    all_to_all x1, waiting for transfers between devices: 6.41 us -> 4.07 us  [body(): lax.all_to_all(to_strips(queries), 'frame', split_axis=0, concat_axis=2,...]
    all_to_all x1, starting transfers between devices: 3.33 us -> 5.19 us  [body(): lax.all_to_all(to_strips(values), 'frame', split_axis=0, concat_axis=2, t...]
    all_to_all x1, starting transfers between devices: 5.04 us -> 3.33 us  [body(): lax.all_to_all(strip_out, 'frame', split_axis=2, concat_axis=0, tiled=True)]
    all_to_all x1, starting transfers between devices: 5.1 us -> 6.35 us  [body(): lax.all_to_all(to_strips(queries), 'frame', split_axis=0, concat_axis=2,...]
    dot_general x1, matrix products: 1.42 us -> 0.45 us  [partial_attend(): jnp.einsum('frd,fnd->frn', query_rows, key_rows, preferred_element_type=j...]
  transfers between devices with their start and end apart: 4 -> 7, of which waited for: 2 -> 4; matrix products, arithmetic and copies ran while one was open for 7% -> 11% of each run, Pallas kernels for 0% -> 0%
where the time goes in v1:
time: 49.9 us; the launch traced here: 49.4 us
  starting transfers between devices  18.6 us (37%)
  waiting for transfers between devices  15.6 us (31%)
  blocking collectives  7.17 us (14%)
  local copies, waits for them, and re-layouts  5.93 us (12%)
  matrix products  1.43 us (3%)
    all_gather x1, blocking collectives, body(): lax.all_gather(value_spatial, ('quarter', 'sub'), axis=1, tiled=True)  7.17 us
    all_to_all x1, starting transfers between devices, body(): lax.all_to_all(to_strips(queries), 'frame', split_axis=0, concat_axis=2,...  6.35 us
    all_to_all x1, waiting for transfers between devices, body(): lax.all_to_all(to_strips(values), 'frame', split_axis=0, concat_axis=2, t...  6.22 us
    all_to_all x1, starting transfers between devices, body(): lax.all_to_all(to_strips(values), 'frame', split_axis=0, concat_axis=2, t...  5.19 us
    all_to_all x1, waiting for transfers between devices, body(): lax.all_to_all(strip_out, 'frame', split_axis=2, concat_axis=0, tiled=True)  5.18 us
    all_to_all x1, waiting for transfers between devices, body(): lax.all_to_all(to_strips(queries), 'frame', split_axis=0, concat_axis=2,...  4.07 us
    all_to_all x1, starting transfers between devices, body(): lax.all_to_all(strip_out, 'frame', split_axis=2, concat_axis=0, tiled=True)  3.33 us
    all_to_all x1, starting transfers between devices, body(): lax.all_to_all(to_strips(keys), 'frame', split_axis=0, concat_axis=2, til...  3.32 us
  transfers between devices with their start and end apart: 7, of which 4 were waited for; matrix products, arithmetic and copies ran while one was open for 11% of the time, Pallas kernels for 0%

profile of v1, /device:TPU:0, one launch (start us, length us, event | category | flops | bytes accessed | tf_op | source)
XLA Modules:
  0.0 49.4 jit_solution(13055516411273821163)
XLA Ops:
  0.0 1.0 %slice.21 = bf16[2,256,128]{2,1,0:T(8,128)(2,1)S(1)} slice(bf16[2,256,256]{2,1,0:T(8,128)(2,1)} %param.3), slice={[0:2], [0:256], [128:256]} | slice | bytes 262144 | tf_op jit(solution)/shard_map/slice | solution.py:75
  1.0 0.7 %copy.33 = bf16[4,4,2,16,128]{4,3,2,1,0:T(8,128)(2,1)} copy(bf16[4,4,2,16,128]{4,3,1,0,2:T(8,128)(2,1)S(1)} %bitcast.50) | data formatting | bytes 262144 | tf_op jit(solution)/shard_map/transpose | solution.py:78
  1.6 6.3 %all-to-all-start = ((bf16[4,4,2,16,128]{4,3,2,1,0:T(8,128)(2,1)}), bf16[4,4,2,16,128]{4,3,2,1,0:T(8,128)(2,1)S(1)}, u32[]{:S(2)}, u32[]{:S(2)}) async-start(bf16[4,4,2,16,128]{4,3,2,1,0:T(8,128)(2,1)} %copy.33), calls=%async_computation | async-start | bytes 262144 | tf_op jit(solution)/shard_map/all_to_all | solution.py:80
  8.0 1.0 %fusion.18 = (bf16[2,256,128]{2,1,0:T(8,128)(2,1)S(1)}, bf16[2,1024,128]{2,1,0:T(8,128)(2,1)S(1)}, bf16[2,256,128]{2,1,0:T(8,128)(2,1)S(1)}) fusion(bf16[2,256,256]{2,1,0:T(8,128)(2,1)} %param.4, bf16[2,1024,128]{2,1,0:T(8,128)(2,1)S(1)} %broadcast_in_dim.7, s32[]{:T(128)S(6)} %select_n.27), kind=kLoop, calls=%fused_computation.27 | loop fusion | bytes 655364 | tf_op jit(solution)/shard_map/slice | solution.py:69
  9.1 0.7 %copy.35 = bf16[4,4,2,16,128]{4,3,2,1,0:T(8,128)(2,1)} copy(bf16[4,4,2,16,128]{4,3,1,0,2:T(8,128)(2,1)S(1)} %bitcast.53) | data formatting | bytes 262144 | tf_op jit(solution)/shard_map/transpose | solution.py:78
  9.9 0.1 copy.48
  10.0 4.1 %all-to-all-done = bf16[4,4,2,16,128]{4,3,2,1,0:T(8,128)(2,1)S(1)} async-done(((bf16[4,4,2,16,128]{4,3,2,1,0:T(8,128)(2,1)}), bf16[4,4,2,16,128]{4,3,2,1,0:T(8,128)(2,1)S(1)}, u32[]{:S(2)}, u32[]{:S(2)}) %all-to-all-start) | async-done | bytes 131104 | tf_op jit(solution)/shard_map/all_to_all | solution.py:80
  14.0 3.3 %all-to-all-start.1 = ((bf16[4,4,2,16,128]{4,3,2,1,0:T(8,128)(2,1)}), bf16[4,4,2,16,128]{4,3,2,1,0:T(8,128)(2,1)S(1)}, u32[]{:S(2)}, u32[]{:S(2)}) async-start(bf16[4,4,2,16,128]{4,3,2,1,0:T(8,128)(2,1)} %copy.35), calls=%async_computation.1 | async-start | bytes 262144 | tf_op jit(solution)/shard_map/all_to_all | solution.py:83
  17.4 7.2 %all_gather.3 = bf16[2,1024,128]{1,2,0:T(8,128)(2,1)S(1)} all-gather(bf16[2,256,128]{1,2,0:T(8,128)(2,1)S(1)} %copy.48), channel_id=1, replica_groups=mesh['groups'=2,'frame'=4,'quarter'=2,'sub'=2] {'quarter','sub'}, dimensions={1}, use_global_device_ids=true | all-gather | bytes 655360 | tf_op jit(solution)/shard_map/all_gather | solution.py:114
  24.6 0.7 %copy.37 = bf16[4,4,2,16,128]{4,3,2,1,0:T(8,128)(2,1)} copy(bf16[4,4,2,16,128]{4,3,1,0,2:T(8,128)(2,1)S(1)} %bitcast.51) | data formatting | bytes 262144 | tf_op jit(solution)/shard_map/transpose | solution.py:78
  25.2 0.3 collective-permute-start.1
  25.6 5.2 %all-to-all-start.2 = ((bf16[4,4,2,16,128]{4,3,2,1,0:T(8,128)(2,1)}), bf16[4,4,2,16,128]{4,3,2,1,0:T(8,128)(2,1)S(1)}, u32[]{:S(2)}, u32[]{:S(2)}) async-start(bf16[4,4,2,16,128]{4,3,2,1,0:T(8,128)(2,1)} %copy.37), calls=%async_computation.2 | async-start | bytes 262144 | tf_op jit(solution)/shard_map/all_to_all | solution.py:84
  30.8 0.2 fusion.19
  31.0 6.2 %all-to-all-done.2 = bf16[4,4,2,16,128]{4,3,2,1,0:T(8,128)(2,1)S(1)} async-done(((bf16[4,4,2,16,128]{4,3,2,1,0:T(8,128)(2,1)}), bf16[4,4,2,16,128]{4,3,2,1,0:T(8,128)(2,1)S(1)}, u32[]{:S(2)}, u32[]{:S(2)}) %all-to-all-start.2) | async-done | bytes 131104 | tf_op jit(solution)/shard_map/all_to_all | solution.py:84
  37.4 0.2 fusion.3
  37.7 0.7 %copy.40 = bf16[1,4,8,16,128]{4,3,1,0,2:T(8,128)(2,1)} copy(bf16[1,4,8,16,128]{4,3,2,1,0:T(8,128)(2,1)S(1)} %bitcast.56) | data formatting | bytes 262144 | tf_op jit(solution)/shard_map/reshape | solution.py:104
  38.3 3.3 %all-to-all-start.3 = ((bf16[1,4,8,16,128]{4,3,1,0,2:T(8,128)(2,1)}), bf16[1,4,8,16,128]{4,3,1,0,2:T(8,128)(2,1)S(1)}, u32[]{:S(2)}, u32[]{:S(2)}) async-start(bf16[1,4,8,16,128]{4,3,1,0,2:T(8,128)(2,1)} %copy.40), calls=%async_computation.3 | async-start | bytes 262144 | tf_op jit(solution)/shard_map/all_to_all | solution.py:106
  41.7 0.1 collective-permute-done.2
  41.8 0.4 bitcast_reduce_fusion
  42.3 0.4 fusion.1
  42.7 0.5 %divide_convert_fusion = bf16[2,256,128]{1,2,0:T(8,128)(2,1)S(1)} fusion(f32[2,256]{1,0:T(2,128)S(1)} %get-tuple-element.11, bf16[2,1024,128]{1,2,0:T(8,128)(2,1)S(1)} %all_gather.3, f32[2,1024,256]{2,1,0:T(8,128)S(1)} %get-tuple-element.15, f32[2,256]{1,0:T(2,128)S(1)} %get-tuple-element.14, f32[2,256]{1,0:T(2,128)S(1)} %get-tuple-element.10), kind=kOutput, calls=%fused_computation.13 | convolution fusion | flops 135987200 | bytes 2758656 | tf_op jit(solution)/shard_map/frn,fnd->frd/dot_general | solution.py:32
  43.2 5.2 %all-to-all-done.3 = bf16[1,4,8,16,128]{4,3,1,0,2:T(8,128)(2,1)S(1)} async-done(((bf16[1,4,8,16,128]{4,3,1,0,2:T(8,128)(2,1)}), bf16[1,4,8,16,128]{4,3,1,0,2:T(8,128)(2,1)S(1)}, u32[]{:S(2)}, u32[]{:S(2)}) %all-to-all-start.3) | async-done | bytes 131104 | tf_op jit(solution)/shard_map/all_to_all | solution.py:106
  48.4 0.1 copy.43
  48.5 0.8 %copy.44 = bf16[2,256,256]{2,1,0:T(8,128)(2,1)} copy(bf16[2,256,256]{1,2,0:T(8,128)(2,1)S(1)} %pad_maximum_fusion) | data formatting | bytes 524288 | tf_op jit(solution)/shard_map/concatenate | solution.py:118
  (21 shorter events, 0.4 us)
Async XLA Ops:
  0.0 9.8 %copy-start.1 = (bf16[2,256,256]{2,1,0:T(8,128)(2,1)S(1)}, bf16[2,256,256]{2,1,0:T(8,128)(2,1)}, u32[]{:S(2)}) copy-start(bf16[2,256,256]{2,1,0:T(8,128)(2,1)} %param.5) | copy-start | bytes 786436
  1.6 12.4 %all-to-all-start = ((bf16[4,4,2,16,128]{4,3,2,1,0:T(8,128)(2,1)}), bf16[4,4,2,16,128]{4,3,2,1,0:T(8,128)(2,1)S(1)}, u32[]{:S(2)}, u32[]{:S(2)}) async-start(bf16[4,4,2,16,128]{4,3,2,1,0:T(8,128)(2,1)} %copy.33), calls=%async_computation | async-start | bytes 262144 | tf_op jit(solution)/shard_map/all_to_all | solution.py:80
  9.1 16.1 %collective-permute-start = (bf16[2,256,128]{2,1,0:T(8,128)(2,1)S(1)}, bf16[2,256,128]{2,1,0:T(8,128)(2,1)S(1)}, u32[]{:S(2)}, u32[]{:S(2)}) collective-permute-start(bf16[2,256,128]{2,1,0:T(8,128)(2,1)S(1)} %get-tuple-element.7), channel_id=1, source_target_pairs={{0,1},{1,2},{2,3},{3,0},{4,5},{5,6},{6,7},{7,4},{8,9},{9,10},{10,1... | collective-permute-start | bytes 393224 | tf_op jit(solution)/shard_map/ppermute | solution.py:17
  14.0 11.6 %all-to-all-start.1 = ((bf16[4,4,2,16,128]{4,3,2,1,0:T(8,128)(2,1)}), bf16[4,4,2,16,128]{4,3,2,1,0:T(8,128)(2,1)S(1)}, u32[]{:S(2)}, u32[]{:S(2)}) async-start(bf16[4,4,2,16,128]{4,3,2,1,0:T(8,128)(2,1)} %copy.35), calls=%async_computation.1 | async-start | bytes 262144 | tf_op jit(solution)/shard_map/all_to_all | solution.py:83
  25.2 12.1 %collective-permute-start.1 = (bf16[2,256,128]{2,1,0:T(8,128)(2,1)S(1)}, bf16[2,256,128]{2,1,0:T(8,128)(2,1)S(1)}, u32[]{:S(2)}, u32[]{:S(2)}) collective-permute-start(bf16[2,256,128]{2,1,0:T(8,128)(2,1)S(1)} %collective-permute-done), channel_id=1, source_target_pairs={{0,1},{1,2},{2,3},{3,0},{4,5},{5,6},{6,7},{7,4},{8,9},{9,10},{10,1... | collective-permute-start | bytes 393224 | tf_op jit(solution)/shard_map/ppermute | solution.py:17
  25.6 16.3 %copy-start = (bf16[2,256,256]{2,1,0:T(8,128)(2,1)S(1)}, bf16[2,256,256]{2,1,0:T(8,128)(2,1)}, u32[]{:S(2)}) copy-start(bf16[2,256,256]{2,1,0:T(8,128)(2,1)} %param.3) | copy-start | bytes 786436
  25.6 11.7 %all-to-all-start.2 = ((bf16[4,4,2,16,128]{4,3,2,1,0:T(8,128)(2,1)}), bf16[4,4,2,16,128]{4,3,2,1,0:T(8,128)(2,1)S(1)}, u32[]{:S(2)}, u32[]{:S(2)}) async-start(bf16[4,4,2,16,128]{4,3,2,1,0:T(8,128)(2,1)} %copy.37), calls=%async_computation.2 | async-start | bytes 262144 | tf_op jit(solution)/shard_map/all_to_all | solution.py:84
  37.4 4.4 %collective-permute-start.2 = (bf16[2,256,128]{2,1,0:T(8,128)(2,1)S(1)}, bf16[2,256,128]{2,1,0:T(8,128)(2,1)S(1)}, u32[]{:S(2)}, u32[]{:S(2)}) collective-permute-start(bf16[2,256,128]{2,1,0:T(8,128)(2,1)S(1)} %collective-permute-done.1), channel_id=1, source_target_pairs={{0,1},{1,2},{2,3},{3,0},{4,5},{5,6},{6,7},{7,4},{8,9},{9,10},{10,1... | collective-permute-start | bytes 393224 | tf_op jit(solution)/shard_map/ppermute | solution.py:17
  38.3 10.0 %all-to-all-start.3 = ((bf16[1,4,8,16,128]{4,3,1,0,2:T(8,128)(2,1)}), bf16[1,4,8,16,128]{4,3,1,0,2:T(8,128)(2,1)S(1)}, u32[]{:S(2)}, u32[]{:S(2)}) async-start(bf16[1,4,8,16,128]{4,3,1,0,2:T(8,128)(2,1)} %copy.40), calls=%async_computation.3 | async-start | bytes 262144 | tf_op jit(solution)/shard_map/all_to_all | solution.py:106
